TPU v7x, 32 devices: a whole 2x2x4 slice. The times are simulated.
32 devices in a mesh: ctx: 16 (over z, x, core), fsdp: 2 (over y).
Axes of the slice: x: 2, y: 2, z: 4, core: 2. Of those that a mesh axis runs over, the one named last changes fastest.
Arguments:
- tokens: bfloat16 [2, 4096, 768], P('fsdp', 'ctx'), may hold values from -6 to 6
- query_weight: bfloat16 [768, 768], P('fsdp'), may hold values from -0.21875 to 0.21875
- query_bias: bfloat16 [768], P('fsdp'), may hold values from -1.5 to 1.5
- key_weight: bfloat16 [768, 768], P('fsdp'), may hold values from -0.21875 to 0.21875
- value_weight: bfloat16 [768, 768], P('fsdp'), may hold values from -0.21875 to 0.21875
- value_bias: bfloat16 [768], P('fsdp'), may hold values from -1.5 to 1.5
- out_weight: bfloat16 [768, 768], P('fsdp'), may hold values from -1.25 to 1.25
- out_bias: bfloat16 [768], P('fsdp'), may hold values from -1.5 to 1.5
- first_gain: bfloat16 [768], P('fsdp'), may hold values from 0.5 to 1.5
- first_shift: bfloat16 [768], P('fsdp'), may hold values from -1.5 to 1.5
- inner_weight: bfloat16 [768, 3072], P('fsdp'), may hold values from -0.21875 to 0.21875
- inner_bias: bfloat16 [3072], P('fsdp'), may hold values from -1.5 to 1.5
- outer_weight: bfloat16 [3072, 768], P('fsdp'), may hold values from -0.109375 to 0.109375
- outer_bias: bfloat16 [768], P('fsdp'), may hold values from -1.5 to 1.5
- second_gain: bfloat16 [768], P('fsdp'), may hold values from 0.5 to 1.5
- second_shift: bfloat16 [768], P('fsdp'), may hold values from -1.5 to 1.5
- doc_lengths: int32 [2, 48], P('fsdp'), may hold values from 1 to 2304, 4096 in all within a row
- grad_output: bfloat16 [2, 4096, 768], P('fsdp', 'ctx'), may hold values from -6 to 6
Outputs:
- output: bfloat16 [2, 4096, 768], P('fsdp', 'ctx')
- grad_tokens: float32 [2, 4096, 768], P('fsdp', 'ctx')
- grad_query_weight: float32 [768, 768], P('fsdp')
- grad_query_bias: float32 [768], P('fsdp')
- grad_key_weight: float32 [768, 768], P('fsdp')
- grad_value_weight: float32 [768, 768], P('fsdp')
- grad_value_bias: float32 [768], P('fsdp')
- grad_out_weight: float32 [768, 768], P('fsdp')
- grad_out_bias: float32 [768], P('fsdp')
- grad_first_gain: float32 [768], P('fsdp')
- grad_first_shift: float32 [768], P('fsdp')
- grad_inner_weight: float32 [768, 3072], P('fsdp')
- grad_inner_bias: float32 [3072], P('fsdp')
- grad_outer_weight: float32 [3072, 768], P('fsdp')
- grad_outer_bias: float32 [768], P('fsdp')
- grad_second_gain: float32 [768], P('fsdp')
- grad_second_shift: float32 [768], P('fsdp')
Inputs may be any that keep to these rules, and one draw needn't show every extreme that they name: `doc_lengths`: each row holds the 48 document lengths of one sequence in order; they sum to 4096 and the longest is exactly 2304.
All inputs are finite; a program needn't handle non-finite values.
Results may differ from a plain program's by a relative error of at most 0.018.
Values may be sent and summed in bfloat16 or wider, within the bound.
No kernel may reach another device: no remote copies, remote signals or barrier semaphores. Data moves between devices by JAX's collectives and lax.ppermute only.
A program may use at most 384 MiB of HBM per device.

v0:
```python
import math
import jax
import jax.numpy as jnp
from jax import lax
from jax.sharding import PartitionSpec as P

H = 12
HD = 64
eps = 1e-12


def layer_norm(r, gain, shift):
    mean = jnp.mean(r, axis=-1, keepdims=True)
    centered = r - mean
    var = jnp.mean(centered * centered, axis=-1, keepdims=True)
    return centered * lax.rsqrt(var + eps) * gain + shift


def gelu_exact(v):
    return jax.nn.gelu(v, approximate=False)


def inner_rows(left, right):
    return lax.dot_general(
        left, right, (((1,), (1,)), ((), ())), preferred_element_type=jnp.float32
    )


def inner_cols(left, right):
    return lax.dot_general(
        left, right, (((0,), (0,)), ((), ())), preferred_element_type=jnp.float32
    )


def segment_of(places, lengths):
    ends = jnp.cumsum(lengths)
    return jnp.sum((places[:, None] >= ends[None, :]).astype(jnp.int32), axis=1)


def masked_scores(query_part, key_part, allowed, scale):
    raw = inner_rows(query_part, key_part) * scale
    return jnp.where(allowed, raw, jnp.float32(-1e30))


def on_device(
    tokens,
    query_weight,
    query_bias,
    key_weight,
    value_weight,
    value_bias,
    out_weight,
    out_bias,
    first_gain,
    first_shift,
    inner_weight,
    inner_bias,
    outer_weight,
    outer_bias,
    second_gain,
    second_shift,
    doc_lengths,
    grad_output,
):
    rows = tokens.shape[1]
    width = tokens.shape[2]
    scale = 1.0 / math.sqrt(HD)
    length_total = rows * lax.axis_size("ctx")
    gathered = (
        lax.all_gather(query_weight, "fsdp", axis=0, tiled=True),
        lax.all_gather(query_bias, "fsdp", axis=0, tiled=True),
        lax.all_gather(key_weight, "fsdp", axis=0, tiled=True),
        lax.all_gather(value_weight, "fsdp", axis=0, tiled=True),
        lax.all_gather(value_bias, "fsdp", axis=0, tiled=True),
        lax.all_gather(out_weight, "fsdp", axis=0, tiled=True),
        lax.all_gather(out_bias, "fsdp", axis=0, tiled=True),
        lax.all_gather(first_gain, "fsdp", axis=0, tiled=True),
        lax.all_gather(first_shift, "fsdp", axis=0, tiled=True),
        lax.all_gather(inner_weight, "fsdp", axis=0, tiled=True),
        lax.all_gather(inner_bias, "fsdp", axis=0, tiled=True),
        lax.all_gather(outer_weight, "fsdp", axis=0, tiled=True),
        lax.all_gather(outer_bias, "fsdp", axis=0, tiled=True),
        lax.all_gather(second_gain, "fsdp", axis=0, tiled=True),
        lax.all_gather(second_shift, "fsdp", axis=0, tiled=True),
    )
    (
        query_full,
        qbias_full,
        key_full,
        value_full,
        vbias_full,
        out_full,
        obias_full,
        gain_one,
        shift_one,
        inner_full,
        ibias_full,
        outer_full,
        outbias_full,
        gain_two,
        shift_two,
    ) = gathered
    local_in = tokens[0]
    local_float = local_in.astype(jnp.float32)
    query_low = (
        jnp.dot(local_in, query_full, preferred_element_type=jnp.float32)
        + qbias_full.astype(jnp.float32)
    ).astype(jnp.bfloat16)
    key_low = jnp.dot(local_in, key_full, preferred_element_type=jnp.float32).astype(jnp.bfloat16)
    value_low = (
        jnp.dot(local_in, value_full, preferred_element_type=jnp.float32)
        + vbias_full.astype(jnp.float32)
    ).astype(jnp.bfloat16)
    first_row = lax.axis_index("ctx") * rows
    places_own = first_row + jnp.arange(rows, dtype=jnp.int32)
    segs_own = segment_of(places_own, doc_lengths[0])
    keys_all, values_all = (
        lax.all_gather(key_low, "ctx", axis=0, tiled=True),
        lax.all_gather(value_low, "ctx", axis=0, tiled=True),
    )
    places_all = jnp.arange(length_total, dtype=jnp.int32)
    segs_all = segment_of(places_all, doc_lengths[0])
    allowed = segs_own[:, None] == segs_all[None, :]
    head_outs = []
    log_list = []
    for head in range(H):
        cols = slice(head * HD, (head + 1) * HD)
        scores = masked_scores(query_low[:, cols], keys_all[:, cols], allowed, scale)
        top = jnp.max(scores, axis=1, keepdims=True)
        expd = jnp.exp(scores - top)
        total = jnp.sum(expd, axis=1, keepdims=True)
        probs_low = (expd / total).astype(jnp.bfloat16)
        head_outs.append(
            jnp.dot(probs_low, values_all[:, cols], preferred_element_type=jnp.float32)
        )
        log_list.append(top[:, 0] + jnp.log(total[:, 0]))
    attn_low = jnp.concatenate(head_outs, axis=1).astype(jnp.bfloat16)
    log_sums = jnp.stack(log_list, axis=0)
    branch = jnp.dot(attn_low, out_full, preferred_element_type=jnp.float32) + obias_full.astype(
        jnp.float32
    )
    hidden, first_back = jax.vjp(
        layer_norm,
        local_float + branch,
        gain_one.astype(jnp.float32),
        shift_one.astype(jnp.float32),
    )
    hidden_low = hidden.astype(jnp.bfloat16)
    inner = jnp.dot(hidden_low, inner_full, preferred_element_type=jnp.float32) + ibias_full.astype(
        jnp.float32
    )
    active, gelu_back = jax.vjp(gelu_exact, inner)
    active_low = active.astype(jnp.bfloat16)
    outer = jnp.dot(
        active_low, outer_full, preferred_element_type=jnp.float32
    ) + outbias_full.astype(jnp.float32)
    result, second_back = jax.vjp(
        layer_norm, hidden + outer, gain_two.astype(jnp.float32), shift_two.astype(jnp.float32)
    )
    output = result.astype(jnp.bfloat16)[None]
    grad_y = grad_output[0].astype(jnp.float32)
    d_second, grad_gain_two, grad_shift_two = second_back(grad_y)
    d_outer_low = d_second.astype(jnp.bfloat16)
    grad_outbias = jnp.sum(d_outer_low.astype(jnp.float32), axis=0)
    grad_outer = inner_cols(active_low, d_outer_low)
    d_active = inner_rows(d_outer_low, outer_full)
    (d_inner,) = gelu_back(d_active)
    d_inner_low = d_inner.astype(jnp.bfloat16)
    grad_ibias = jnp.sum(d_inner_low.astype(jnp.float32), axis=0)
    grad_inner = inner_cols(hidden_low, d_inner_low)
    d_hidden = d_second + inner_rows(d_inner_low, inner_full)
    d_first, grad_gain_one, grad_shift_one = first_back(d_hidden)
    d_branch_low = d_first.astype(jnp.bfloat16)
    grad_obias = jnp.sum(d_branch_low.astype(jnp.float32), axis=0)
    grad_out = inner_cols(attn_low, d_branch_low)
    d_attn_low = inner_rows(d_branch_low, out_full).astype(jnp.bfloat16)
    dq_list = []
    dk_list = []
    dv_list = []
    for head in range(H):
        cols = slice(head * HD, (head + 1) * HD)
        scores = masked_scores(query_low[:, cols], keys_all[:, cols], allowed, scale)
        probs = jnp.exp(scores - log_sums[head][:, None])
        d_probs = inner_rows(d_attn_low[:, cols], values_all[:, cols])
        delta = jnp.sum(probs * d_probs, axis=1)
        d_scores = (probs * (d_probs - delta[:, None])).astype(jnp.bfloat16)
        dq_list.append(
            jnp.dot(d_scores, keys_all[:, cols], preferred_element_type=jnp.float32) * scale
        )
        dk_list.append(inner_cols(d_scores, query_low[:, cols]) * scale)
        dv_list.append(inner_cols(probs.astype(jnp.bfloat16), d_attn_low[:, cols]))
    key_terms = jnp.concatenate(dk_list + dv_list, axis=1)
    shares = lax.psum_scatter(
        key_terms.astype(jnp.bfloat16), "ctx", scatter_dimension=0, tiled=True
    ).astype(jnp.float32)
    d_key_low = shares[:, :width].astype(jnp.bfloat16)
    d_value_low = shares[:, width:].astype(jnp.bfloat16)
    d_query_low = jnp.concatenate(dq_list, axis=1).astype(jnp.bfloat16)
    grad_qbias = jnp.sum(d_query_low.astype(jnp.float32), axis=0)
    grad_vbias = jnp.sum(d_value_low.astype(jnp.float32), axis=0)
    grad_query = inner_cols(local_in, d_query_low)
    grad_key = inner_cols(local_in, d_key_low)
    grad_value = inner_cols(local_in, d_value_low)
    grad_input = (
        d_first
        + inner_rows(d_query_low, query_full)
        + inner_rows(d_key_low, key_full)
        + inner_rows(d_value_low, value_full)
    )
    shards = (
        lax.psum_scatter(
            grad_query.astype(jnp.bfloat16), "fsdp", scatter_dimension=0, tiled=True
        ).astype(jnp.float32),
        lax.psum_scatter(
            grad_qbias.astype(jnp.bfloat16), "fsdp", scatter_dimension=0, tiled=True
        ).astype(jnp.float32),
        lax.psum_scatter(
            grad_key.astype(jnp.bfloat16), "fsdp", scatter_dimension=0, tiled=True
        ).astype(jnp.float32),
        lax.psum_scatter(
            grad_value.astype(jnp.bfloat16), "fsdp", scatter_dimension=0, tiled=True
        ).astype(jnp.float32),
        lax.psum_scatter(
            grad_vbias.astype(jnp.bfloat16), "fsdp", scatter_dimension=0, tiled=True
        ).astype(jnp.float32),
        lax.psum_scatter(
            grad_out.astype(jnp.bfloat16), "fsdp", scatter_dimension=0, tiled=True
        ).astype(jnp.float32),
        lax.psum_scatter(
            grad_obias.astype(jnp.bfloat16), "fsdp", scatter_dimension=0, tiled=True
        ).astype(jnp.float32),
        lax.psum_scatter(
            grad_gain_one.astype(jnp.bfloat16), "fsdp", scatter_dimension=0, tiled=True
        ).astype(jnp.float32),
        lax.psum_scatter(
            grad_shift_one.astype(jnp.bfloat16), "fsdp", scatter_dimension=0, tiled=True
        ).astype(jnp.float32),
        lax.psum_scatter(
            grad_inner.astype(jnp.bfloat16), "fsdp", scatter_dimension=0, tiled=True
        ).astype(jnp.float32),
        lax.psum_scatter(
            grad_ibias.astype(jnp.bfloat16), "fsdp", scatter_dimension=0, tiled=True
        ).astype(jnp.float32),
        lax.psum_scatter(
            grad_outer.astype(jnp.bfloat16), "fsdp", scatter_dimension=0, tiled=True
        ).astype(jnp.float32),
        lax.psum_scatter(
            grad_outbias.astype(jnp.bfloat16), "fsdp", scatter_dimension=0, tiled=True
        ).astype(jnp.float32),
        lax.psum_scatter(
            grad_gain_two.astype(jnp.bfloat16), "fsdp", scatter_dimension=0, tiled=True
        ).astype(jnp.float32),
        lax.psum_scatter(
            grad_shift_two.astype(jnp.bfloat16), "fsdp", scatter_dimension=0, tiled=True
        ).astype(jnp.float32),
    )
    totals = lax.psum(tuple(shards), "ctx")
    return (output, grad_input[None]) + tuple(totals)


def solution(mesh):
    placed = (
        P("fsdp", "ctx", None),
        P("fsdp", None),
        P("fsdp"),
        P("fsdp", None),
        P("fsdp", None),
        P("fsdp"),
        P("fsdp", None),
        P("fsdp"),
        P("fsdp"),
        P("fsdp"),
        P("fsdp", None),
        P("fsdp"),
        P("fsdp", None),
        P("fsdp"),
        P("fsdp"),
        P("fsdp"),
        P("fsdp", None),
        P("fsdp", "ctx", None),
    )
    return jax.shard_map(
        on_device,
        mesh=mesh,
        in_specs=placed,
        out_specs=(
            P("fsdp", "ctx", None),
            P("fsdp", "ctx", None),
            P("fsdp", None),
            P("fsdp"),
            P("fsdp", None),
            P("fsdp", None),
            P("fsdp"),
            P("fsdp", None),
            P("fsdp"),
            P("fsdp"),
            P("fsdp"),
            P("fsdp", None),
            P("fsdp"),
            P("fsdp", None),
            P("fsdp"),
            P("fsdp"),
            P("fsdp"),
        ),
        check_vma=False,
    )
```

profile of v0, /device:TPU:1, one launch (start us, length us, event | category | flops | bytes accessed | tf_op | source)
XLA Modules:
  0.0 1196.2 jit_solution(10272641338332044763)
XLA Ops:
  9.5 25.0 %all-gather.20.cloned.1.call-done = bf16[768,768]{1,0:T(8,128)(2,1)} async-done(((bf16[384,768]{1,0:T(8,128)(2,1)}), bf16[768,768]{1,0:T(8,128)(2,1)}) %all-gather.20.cloned.1.call-update) | async-done | bytes 1179664 | tf_op jit(solution)/shard_map/all_gather | solution.py:72
  41.2 17.6 %all-gather.24.cloned.1.call-done = bf16[768,768]{1,0:T(8,128)(2,1)} async-done(((bf16[384,768]{1,0:T(8,128)(2,1)}), bf16[768,768]{1,0:T(8,128)(2,1)}) %all-gather.24.cloned.1.call-update) | async-done | bytes 1179664 | tf_op jit(solution)/shard_map/all_gather | solution.py:73
  93.4 54.9 %all-gather.22.cloned.1.call-done = bf16[4096,768]{1,0:T(8,128)(2,1)} async-done(((bf16[256,768]{1,0:T(8,128)(2,1)}), bf16[4096,768]{1,0:T(8,128)(2,1)}) %all-gather.22.cloned.1.call-update) | async-done | bytes 6291472 | tf_op jit(solution)/shard_map/all_gather | solution.py:118
  194.7 16.8 %all-gather.26.cloned.1.call-done = bf16[4096,768]{1,0:T(8,128)(2,1)} async-done(((bf16[256,768]{1,0:T(8,128)(2,1)}), bf16[4096,768]{1,0:T(8,128)(2,1)}) %all-gather.26.cloned.1.call-update) | async-done | bytes 6291472 | tf_op jit(solution)/shard_map/all_gather | solution.py:119
  243.4 54.8 %all-gather.30.cloned.1.call-done = bf16[768,3072]{1,0:T(8,128)(2,1)} async-done(((bf16[384,3072]{1,0:T(8,128)(2,1)}), bf16[768,3072]{1,0:T(8,128)(2,1)}) %all-gather.30.cloned.1.call-update) | async-done | bytes 4718608 | tf_op jit(solution)/shard_map/all_gather | solution.py:79
  298.2 11.5 multiply_convert_fusion.12
  309.7 52.7 %all-gather.32.cloned.1.call-done = bf16[3072,768]{1,0:T(8,128)(2,1)} async-done(((bf16[1536,768]{1,0:T(8,128)(2,1)}), bf16[3072,768]{1,0:T(8,128)(2,1)}) %all-gather.32.cloned.1.call-update) | async-done | bytes 4718608 | tf_op jit(solution)/shard_map/all_gather | solution.py:81
  423.8 5.6 multiply_reduce_fusion.4
  429.4 6.4 multiply_convert_fusion.4
  441.1 6.0 multiply_convert_fusion.3
  447.1 5.6 multiply_reduce_fusion.2
  452.6 5.9 multiply_convert_fusion.2
  463.9 6.0 multiply_convert_fusion.1
  469.9 5.6 multiply_reduce_fusion
  475.5 5.9 multiply_convert_fusion
  560.3 93.9 %reduce-scatter.14.cloned.1.call-done = bf16[256,1536]{0,1:T(8,128)(2,1)} async-done(((bf16[4096,1536]{0,1:T(8,128)(2,1)}), bf16[256,1536]{0,1:T(8,128)(2,1)}) %reduce-scatter.14.cloned.1.call-update) | async-done | bytes 786448 | tf_op jit(solution)/shard_map/reduce_scatter | solution.py:193
  668.9 9.7 reduce-scatter.22.cloned.1.call-done
  679.9 22.8 %reduce-scatter.16.cloned.1.call-done = bf16[384,768]{1,0:T(8,128)(2,1)} async-done(((bf16[768,768]{1,0:T(8,128)(2,1)}), bf16[384,768]{1,0:T(8,128)(2,1)}) %reduce-scatter.16.cloned.1.call-update) | async-done | bytes 589840 | tf_op jit(solution)/shard_map/reduce_scatter | solution.py:226
  702.7 62.7 %reduce-scatter.18.cloned.1.call-done = bf16[384,3072]{1,0:T(8,128)(2,1)} async-done(((bf16[768,3072]{1,0:T(8,128)(2,1)}), bf16[384,3072]{1,0:T(8,128)(2,1)}) %reduce-scatter.18.cloned.1.call-update) | async-done | bytes 2359312 | tf_op jit(solution)/shard_map/reduce_scatter | solution.py:238
  765.4 63.0 %reduce-scatter.20.cloned.1.call-done = bf16[1536,768]{1,0:T(8,128)(2,1)} async-done(((bf16[3072,768]{1,0:T(8,128)(2,1)}), bf16[1536,768]{1,0:T(8,128)(2,1)}) %reduce-scatter.20.cloned.1.call-update) | async-done | bytes 2359312 | tf_op jit(solution)/shard_map/reduce_scatter | solution.py:244
  828.6 6.1 all-reduce.10
  841.4 11.6 reduce-scatter.24.cloned.1.call-done
  854.4 23.1 %reduce-scatter.26.cloned.1.call-done = bf16[384,768]{1,0:T(8,128)(2,1)} async-done(((bf16[768,768]{1,0:T(8,128)(2,1)}), bf16[384,768]{1,0:T(8,128)(2,1)}) %reduce-scatter.26.cloned.1.call-update) | async-done | bytes 589840
  878.8 303.9 %all-reduce.12 = (f32[384,768]{0,1:T(8,128)}, f32[384]{0:T(512)}, f32[384,768]{0,1:T(8,128)}, f32[384,768]{0,1:T(8,128)S(1)}, f32[384]{0:T(512)}, /*index=5*/f32...) all-reduce(bf16[384,768]{0,1:T(8,128)(2,1)S(1)} %copy.52, ...), channel_id=1, replica_groups=mesh['ctx'=16,'fsdp'=2] {'ctx'}, use_global_device_ids=true, to_apply=%region_49.50 | all-reduce | flops 3543552 | bytes 21270528 | tf_op jit(solution)/shard_map/psum | solution.py:257
  (427 shorter events, 302.6 us)
Async XLA Ops:
  7.2 27.3 %all-gather.20.cloned.1.call-start = ((), (), s32[]{:S(2)}) async-start(), calls=%async_computation.8 | async-start | bytes 1769472 | tf_op jit(solution)/shard_map/all_gather | solution.py:72
  7.9 50.9 %all-gather.24.cloned.1.call-start = ((), (), s32[]{:S(2)}) async-start(), calls=%async_computation.10 | async-start | bytes 1769472 | tf_op jit(solution)/shard_map/all_gather | solution.py:73
  8.7 82.9 %all-gather.18.cloned.1.call-start = ((), (), s32[]{:S(2)}) async-start(), calls=%async_computation.7 | async-start | bytes 1769472 | tf_op jit(solution)/shard_map/all_gather | solution.py:70
  9.4 138.9 %all-gather.22.cloned.1.call-start = ((), (), s32[]{:S(2)}) async-start(), calls=%async_computation.9 | async-start | bytes 6684672 | tf_op jit(solution)/shard_map/all_gather | solution.py:118
  37.1 40.7 %copy-start.85 = (bf16[384]{0:T(512)(128)(2,1)S(1)}, bf16[384]{0:T(512)(128)(2,1)}, u32[]{:S(2)}) copy-start(bf16[384]{0:T(512)(128)(2,1)} %param.27) | copy-start | bytes 2308
  37.1 44.2 %copy-start.86 = (bf16[384]{0:T(512)(128)(2,1)S(1)}, bf16[384]{0:T(512)(128)(2,1)}, u32[]{:S(2)}) copy-start(bf16[384]{0:T(512)(128)(2,1)} %param.26) | copy-start | bytes 2308
  37.2 47.4 %copy-start.87 = (bf16[384]{0:T(512)(128)(2,1)S(1)}, bf16[384]{0:T(512)(128)(2,1)}, u32[]{:S(2)}) copy-start(bf16[384]{0:T(512)(128)(2,1)} %param.32) | copy-start | bytes 2308
  37.2 50.7 %copy-start.88 = (bf16[384]{0:T(512)(128)(2,1)S(1)}, bf16[384]{0:T(512)(128)(2,1)}, u32[]{:S(2)}) copy-start(bf16[384]{0:T(512)(128)(2,1)} %param.33) | copy-start | bytes 2308
  37.2 54.4 %copy-start.57 = (bf16[1,256,768]{2,1,0:T(8,128)(2,1)S(1)}, bf16[1,256,768]{2,1,0:T(8,128)(2,1)}, u32[]{:S(2)}) copy-start(bf16[1,256,768]{2,1,0:T(8,128)(2,1)} %param.18) | copy-start | bytes 1179652
  37.2 174.3 %all-gather.26.cloned.1.call-start = ((), (), s32[]{:S(2)}) async-start(), calls=%async_computation.11 | async-start | bytes 6684672 | tf_op jit(solution)/shard_map/all_gather | solution.py:119
  61.5 179.4 %all-gather.28.cloned.1.call-start = ((), (), s32[]{:S(2)}) async-start(), calls=%async_computation.12 | async-start | bytes 1769472 | tf_op jit(solution)/shard_map/all_gather | solution.py:75
  62.0 236.2 %all-gather.30.cloned.1.call-start = ((), (), s32[]{:S(2)}) async-start(), calls=%async_computation.13 | async-start | bytes 7077888 | tf_op jit(solution)/shard_map/all_gather | solution.py:79
  62.8 299.6 %all-gather.32.cloned.1.call-start = ((), (), s32[]{:S(2)}) async-start(), calls=%async_computation.14 | async-start | bytes 7077888 | tf_op jit(solution)/shard_map/all_gather | solution.py:81
  63.5 590.6 %reduce-scatter.14.cloned.1.call-start = ((), (), s32[]{:S(2)}) async-start(), calls=%async_computation.15 | async-start | bytes 13369344 | tf_op jit(solution)/shard_map/reduce_scatter | solution.py:193
  93.4 57.8 %copy-start.78 = (bf16[256,768]{1,0:T(8,128)(2,1)}, bf16[256,768]{1,0:T(8,128)(2,1)S(1)}, u32[]{:S(2)}) copy-start(bf16[256,768]{1,0:T(8,128)(2,1)S(1)} %fusion.108) | copy-start | bytes 1179652
  240.9 57.3 %copy-start.75 = (bf16[256,768]{0,1:T(8,128)(2,1)}, bf16[256,768]{0,1:T(8,128)(2,1)S(1)}, u32[]{:S(2)}) copy-start(bf16[256,768]{0,1:T(8,128)(2,1)S(1)} %fusion.157) | copy-start | bytes 1179652
  309.7 56.7 %copy-start.69 = (bf16[256,3072]{1,0:T(8,128)(2,1)}, bf16[256,3072]{1,0:T(8,128)(2,1)S(1)}, u32[]{:S(2)}) copy-start(bf16[256,3072]{1,0:T(8,128)(2,1)S(1)} %get-tuple-element.124) | copy-start | bytes 4718596
  520.1 158.4 %reduce-scatter.22.cloned.1.call-start = ((), (), s32[]{:S(2)}) async-start(), calls=%async_computation.19 | async-start | bytes 1769472
  547.7 155.0 %reduce-scatter.16.cloned.1.call-start = ((), (), s32[]{:S(2)}) async-start(), calls=%async_computation.16 | async-start | bytes 1769472 | tf_op jit(solution)/shard_map/reduce_scatter | solution.py:226
  549.3 216.1 %reduce-scatter.18.cloned.1.call-start = ((), (), s32[]{:S(2)}) async-start(), calls=%async_computation.17 | async-start | bytes 7077888 | tf_op jit(solution)/shard_map/reduce_scatter | solution.py:238
  554.6 273.9 %reduce-scatter.20.cloned.1.call-start = ((), (), s32[]{:S(2)}) async-start(), calls=%async_computation.18 | async-start | bytes 7077888 | tf_op jit(solution)/shard_map/reduce_scatter | solution.py:244
  560.2 292.7 %reduce-scatter.24.cloned.1.call-start = ((), (), s32[]{:S(2)}) async-start(), calls=%async_computation.20 | async-start | bytes 1769472
  657.2 220.3 %reduce-scatter.26.cloned.1.call-start = ((), (), s32[]{:S(2)}) async-start(), calls=%async_computation.21 | async-start | bytes 1769472
  658.7 178.1 %copy-start.64 = (bf16[768,768]{1,0:T(8,128)(2,1)S(1)}, bf16[768,768]{1,0:T(8,128)(2,1)}, u32[]{:S(2)}) copy-start(bf16[768,768]{1,0:T(8,128)(2,1)} %all-gather.20.cloned.1.call-done) | copy-start | bytes 3538948
  (91 other events, 597.9 us)
Sparse Core Ops, SparseCore 0:
  9.6 24.8 all-gather.19
  36.0 22.7 all-gather.23
  60.4 22.9 all-gather.17
  86.0 62.2 all-gather.21
  151.0 60.4 all-gather.25
  212.9 20.9 all-gather.27
  235.5 62.6 all-gather.29
  299.7 62.5 all-gather.31
  520.3 133.8 reduce-scatter.13
  656.8 21.6 reduce-scatter.21
  680.9 21.7 reduce-scatter.15
  705.4 59.9 reduce-scatter.17
  768.4 59.9 reduce-scatter.19
  831.1 21.8 reduce-scatter.23
  855.8 21.6 reduce-scatter.25
where the time goes:
time: 1200 us
  waiting for transfers between devices  513 us (43%)
  blocking collectives  340 us (28%)
  matrix products  214 us (18%)
  other arithmetic  72.8 us (6%)
  local copies, waits for them, and re-layouts  38.5 us (3%)
  between operations  16.7 us (1%)
    psum x1, blocking collectives, on_device(): totals = lax.psum(tuple(shards), 'ctx')  304 us
    dot_general x30, matrix products, inner_rows(): lax.dot_general(left, right, (((1,), (1,)), ((), ())), preferred_element_...  94 us
    reduce_scatter x1, waiting for transfers between devices, on_device(): lax.psum_scatter(key_terms.astype(jnp.bfloat16), 'ctx', scatter_dimension...  93.9 us
    reduce_scatter x1, waiting for transfers between devices, on_device(): lax.psum_scatter(grad_outer.astype(jnp.bfloat16), 'fsdp', scatter_dimensi...  63 us
    reduce_scatter x1, waiting for transfers between devices, on_device(): lax.psum_scatter(grad_inner.astype(jnp.bfloat16), 'fsdp', scatter_dimensi...  62.7 us
    convert_element_type x12, other arithmetic, on_device(): d_scores = (probs * (d_probs - delta[:, None])).astype(jnp.bfloat16)  56.2 us
    all_gather x1, waiting for transfers between devices, on_device(): lax.all_gather(key_low, 'ctx', axis=0, tiled=True)  54.9 us
    all_gather x1, waiting for transfers between devices, on_device(): lax.all_gather(inner_weight, 'fsdp', axis=0, tiled=True)  54.8 us
  transfers between devices with their start and end apart: 15, of which 13 were waited for; matrix products, arithmetic and copies ran while one was open for 12% of the time, Pallas kernels for 0%

commit v1 on v0

--- a/solution.py
+++ b/solution.py
@@ -7,6 +7,28 @@
 H = 12
 HD = 64
 eps = 1e-12
+
+
+def joined_along(parts, dim):
+    lengths = list(parts.shape[1:])
+    lengths[dim] *= parts.shape[0]
+    return jnp.moveaxis(parts, 0, dim).reshape(lengths)
+
+
+def ring_gather(x, axis, dim):
+    size = lax.axis_size(axis)
+    pairs = [(i, (i + 1) % size) for i in range(size)]
+    back = [(b, a) for a, b in pairs]
+    lower, upper = ([], [])
+    for step in range(size - 1):
+        if step % 2 == 0:
+            lower.append(lax.ppermute(lower[-1] if lower else x, axis, pairs))
+        else:
+            upper.append(lax.ppermute(upper[-1] if upper else x, axis, back))
+    blocks = jnp.stack([*lower[::-1], x, *upper])
+    shift = lax.axis_index(axis) - len(lower)
+    blocks = blocks[(jnp.arange(size) - shift) % size]
+    return joined_along(blocks, dim)
 
 
 def layer_norm(r, gain, shift):
@@ -115,7 +137,7 @@
     places_own = first_row + jnp.arange(rows, dtype=jnp.int32)
     segs_own = segment_of(places_own, doc_lengths[0])
     keys_all, values_all = (
-        lax.all_gather(key_low, "ctx", axis=0, tiled=True),
+        ring_gather(key_low, "ctx", 0),
         lax.all_gather(value_low, "ctx", axis=0, tiled=True),
     )
     places_all = jnp.arange(length_total, dtype=jnp.int32)

time: 1200 us -> 1130 us (0.942)
  waiting for transfers between devices: 513 us -> 430 us
  matrix products: 214 us -> 186 us
  local copies, waits for them, and re-layouts: 38.5 us -> 64 us
  starting transfers between devices: 1.07 us -> 24.9 us
  other arithmetic: 72.8 us -> 60 us
    all_gather x1 -> x0, waiting for transfers between devices: 54.9 us -> none  [on_device(): lax.all_gather(key_low, 'ctx', axis=0, tiled=True)]
    all_gather x1, waiting for transfers between devices: 54.8 us -> 0.02 us  [on_device(): lax.all_gather(inner_weight, 'fsdp', axis=0, tiled=True)]
    ppermute x0 -> x15, waiting for transfers between devices: none -> 50.8 us  [the longest x8 32.5 us: ring_gather(): lower.append(lax.ppermute(lower[-1] if lower else x, axis, pairs))]
    dot_general x30, matrix products: 94 us -> 66.3 us  [inner_rows(): lax.dot_general(left, right, (((1,), (1,)), ((), ())), preferred_element_...]
    ppermute x0 -> x15, starting transfers between devices: none -> 23.9 us  [the longest x8 20.2 us: ring_gather(): lower.append(lax.ppermute(lower[-1] if lower else x, axis, pairs))]
    convert_element_type x12, other arithmetic: 56.2 us -> 34.9 us  [on_device(): d_scores = (probs * (d_probs - delta[:, None])).astype(jnp.bfloat16)]
    unnamed x219 -> x248, local copies, waits for them, and re-layouts: 38.3 us -> 56.7 us
    all_gather x1, waiting for transfers between devices: 16.8 us -> 0.01 us  [on_device(): lax.all_gather(value_low, 'ctx', axis=0, tiled=True)]
  transfers between devices with their start and end apart: 15 -> 29, of which waited for: 13 -> 19; matrix products, arithmetic and copies ran while one was open for 12% -> 14% of each run, Pallas kernels for 0% -> 0%
where the time goes in v1:
time: 1130 us; the launch traced here: 1120 us
  waiting for transfers between devices  430 us (38%)
  blocking collectives  341 us (30%)
  matrix products  186 us (16%)
  local copies, waits for them, and re-layouts  64 us (6%)
  other arithmetic  60 us (5%)
  starting transfers between devices  24.9 us (2%)
  between operations  16.8 us (1%)
    psum x1, blocking collectives, on_device(): totals = lax.psum(tuple(shards), 'ctx')  304 us
    reduce_scatter x1, waiting for transfers between devices, on_device(): lax.psum_scatter(key_terms.astype(jnp.bfloat16), 'ctx', scatter_dimension...  93.8 us
    dot_general x30, matrix products, inner_rows(): lax.dot_general(left, right, (((1,), (1,)), ((), ())), preferred_element_...  66.3 us
    reduce_scatter x1, waiting for transfers between devices, on_device(): lax.psum_scatter(grad_inner.astype(jnp.bfloat16), 'fsdp', scatter_dimensi...  62.9 us
    reduce_scatter x1, waiting for transfers between devices, on_device(): lax.psum_scatter(grad_outer.astype(jnp.bfloat16), 'fsdp', scatter_dimensi...  62.9 us
    unnamed x248, local copies, waits for them, and re-layouts  56.7 us
    dot_general x30, matrix products, inner_cols(): lax.dot_general(left, right, (((0,), (0,)), ((), ())), preferred_element_...  55.1 us
    unnamed x17, waiting for transfers between devices  48 us
  transfers between devices with their start and end apart: 29, of which 19 were waited for; matrix products, arithmetic and copies ran while one was open for 14% of the time, Pallas kernels for 0%

profile of v1, /device:TPU:1, one launch (start us, length us, event | category | flops | bytes accessed | tf_op | source)
XLA Modules:
  0.0 1122.6 jit_solution(8759589027572472324)
XLA Ops:
  13.9 20.5 %all-gather.21.cloned.1.call-done = bf16[768,768]{1,0:T(8,128)(2,1)} async-done(((bf16[384,768]{1,0:T(8,128)(2,1)}), bf16[768,768]{1,0:T(8,128)(2,1)}) %all-gather.21.cloned.1.call-update) | async-done | bytes 1179664 | tf_op jit(solution)/shard_map/all_gather | solution.py:95
  38.4 20.4 %all-gather.19.cloned.1.call-done = bf16[768,768]{1,0:T(8,128)(2,1)} async-done(((bf16[384,768]{1,0:T(8,128)(2,1)}), bf16[768,768]{1,0:T(8,128)(2,1)}) %all-gather.19.cloned.1.call-update) | async-done | bytes 1179664 | tf_op jit(solution)/shard_map/all_gather | solution.py:94
  62.4 4.7 collective-permute-done
  71.2 7.3 collective-permute-done.1
  81.4 8.5 collective-permute-done.2
  92.8 11.9 %collective-permute-done.3 = bf16[256,768]{1,0:T(8,128)(2,1)} collective-permute-done((bf16[256,768]{1,0:T(8,128)(2,1)S(1)}, bf16[256,768]{1,0:T(8,128)(2,1)}, u32[]{:S(2)}, u32[]{:S(2)}) %collective-permute-start.3) | collective-permute-done | bytes 393248 | tf_op jit(solution)/shard_map/ppermute | solution.py:25
  135.6 7.8 collective-permute-done.11
  159.6 5.8 collective-permute-done.13
  186.0 6.3 gather_fusion
  213.4 5.8 fusion.36
  262.0 11.7 %multiply_convert_fusion.12 = (bf16[256,3072]{1,0:T(8,128)(2,1)S(1)}, f32[256,3072]{1,0:T(8,128)}, f32[256,3072]{1,0:T(8,128)}) fusion(f32[3072]{0:T(1024)S(1)} %bitcast.145, bf16[768,3072]{1,0:T(8,128)(2,1)} %all-gather.27.cloned.1.call-done, f32[256,768]{1,0:T(8,128)S(1)} %get-tuple-element.152, f32[768]{0:T(1024)S(1)} %reshape.329, ...), kind=kOutput, calls=%fused_computation.175 | convolution fusion | flops 1260847104 | bytes 13389824 | tf_op jit(solution)/shard_map/dot_general | solution.py:171
  273.7 47.9 %all-gather.29.cloned.1.call-done = bf16[3072,768]{1,0:T(8,128)(2,1)} async-done(((bf16[1536,768]{1,0:T(8,128)(2,1)}), bf16[3072,768]{1,0:T(8,128)(2,1)}) %all-gather.29.cloned.1.call-update) | async-done | bytes 4718608 | tf_op jit(solution)/shard_map/all_gather | solution.py:103
  393.3 4.9 multiply_convert_fusion.1
  402.6 4.8 multiply_convert_fusion
  475.6 5.2 convolution_convert_fusion.1
  486.5 93.8 %reduce-scatter.14.cloned.1.call-done = bf16[256,1536]{0,1:T(8,128)(2,1)} async-done(((bf16[4096,1536]{0,1:T(8,128)(2,1)}), bf16[256,1536]{0,1:T(8,128)(2,1)}) %reduce-scatter.14.cloned.1.call-update) | async-done | bytes 786448 | tf_op jit(solution)/shard_map/reduce_scatter | solution.py:215
  595.1 9.8 reduce-scatter.22.cloned.1.call-done
  606.3 22.6 %reduce-scatter.16.cloned.1.call-done = bf16[384,768]{1,0:T(8,128)(2,1)} async-done(((bf16[768,768]{1,0:T(8,128)(2,1)}), bf16[384,768]{1,0:T(8,128)(2,1)}) %reduce-scatter.16.cloned.1.call-update) | async-done | bytes 589840 | tf_op jit(solution)/shard_map/reduce_scatter | solution.py:248
  628.9 62.9 %reduce-scatter.18.cloned.1.call-done = bf16[384,3072]{1,0:T(8,128)(2,1)} async-done(((bf16[768,3072]{1,0:T(8,128)(2,1)}), bf16[384,3072]{1,0:T(8,128)(2,1)}) %reduce-scatter.18.cloned.1.call-update) | async-done | bytes 2359312 | tf_op jit(solution)/shard_map/reduce_scatter | solution.py:260
  691.8 62.9 %reduce-scatter.20.cloned.1.call-done = bf16[1536,768]{1,0:T(8,128)(2,1)} async-done(((bf16[3072,768]{1,0:T(8,128)(2,1)}), bf16[1536,768]{1,0:T(8,128)(2,1)}) %reduce-scatter.20.cloned.1.call-update) | async-done | bytes 2359312 | tf_op jit(solution)/shard_map/reduce_scatter | solution.py:266
  754.8 6.1 all-reduce.10
  767.6 11.7 %reduce-scatter.24.cloned.1.call-done = bf16[384,768]{1,0:T(8,128)(2,1)} async-done(((bf16[768,768]{1,0:T(8,128)(2,1)}), bf16[384,768]{1,0:T(8,128)(2,1)}) %reduce-scatter.24.cloned.1.call-update) | async-done | bytes 589840
  780.6 23.2 %reduce-scatter.26.cloned.1.call-done = bf16[384,768]{1,0:T(8,128)(2,1)} async-done(((bf16[768,768]{1,0:T(8,128)(2,1)}), bf16[384,768]{1,0:T(8,128)(2,1)}) %reduce-scatter.26.cloned.1.call-update) | async-done | bytes 589840
  805.2 303.9 %all-reduce.12 = (f32[384,768]{0,1:T(8,128)}, f32[384]{0:T(512)}, f32[384,768]{0,1:T(8,128)}, f32[384,768]{0,1:T(8,128)S(1)}, f32[384]{0:T(512)}, /*index=5*/f32...) all-reduce(bf16[384,768]{0,1:T(8,128)(2,1)S(1)} %copy.52, ...), channel_id=1, replica_groups=mesh['ctx'=16,'fsdp'=2] {'ctx'}, use_global_device_ids=true, to_apply=%region_49.50 | all-reduce | flops 3543552 | bytes 21270528 | tf_op jit(solution)/shard_map/psum | solution.py:279
  (486 shorter events, 335.3 us)
Async XLA Ops:
  7.2 27.3 %all-gather.21.cloned.1.call-start = ((), (), s32[]{:S(2)}) async-start(), calls=%async_computation.9 | async-start | bytes 1769472 | tf_op jit(solution)/shard_map/all_gather | solution.py:95
  7.9 50.9 %all-gather.19.cloned.1.call-start = ((), (), s32[]{:S(2)}) async-start(), calls=%async_computation.8 | async-start | bytes 1769472 | tf_op jit(solution)/shard_map/all_gather | solution.py:94
  8.7 149.1 %all-gather.17.cloned.1.call-start = ((), (), s32[]{:S(2)}) async-start(), calls=%async_computation.7 | async-start | bytes 1769472 | tf_op jit(solution)/shard_map/all_gather | solution.py:92
  9.4 221.2 %all-gather.23.cloned.1.call-start = ((), (), s32[]{:S(2)}) async-start(), calls=%async_computation.10 | async-start | bytes 6684672 | tf_op jit(solution)/shard_map/all_gather | solution.py:141
  37.2 222.5 %all-gather.25.cloned.1.call-start = ((), (), s32[]{:S(2)}) async-start(), calls=%async_computation.11 | async-start | bytes 1769472 | tf_op jit(solution)/shard_map/all_gather | solution.py:97
  37.8 224.1 %all-gather.27.cloned.1.call-start = ((), (), s32[]{:S(2)}) async-start(), calls=%async_computation.12 | async-start | bytes 7077888 | tf_op jit(solution)/shard_map/all_gather | solution.py:101
  38.4 283.3 %all-gather.29.cloned.1.call-start = ((), (), s32[]{:S(2)}) async-start(), calls=%async_computation.13 | async-start | bytes 7077888 | tf_op jit(solution)/shard_map/all_gather | solution.py:103
  69.6 11.8 %collective-permute-start.8 = (bf16[256,768]{1,0:T(8,128)(2,1)S(1)}, bf16[256,768]{1,0:T(8,128)(2,1)S(1)}, u32[]{:S(2)}, u32[]{:S(2)}) collective-permute-start(bf16[256,768]{1,0:T(8,128)(2,1)S(1)} %convolution_convert_fusion.19), channel_id=1, source_target_pairs={{2,0},{4,2},{6,4},{8,6},{10,8},{12,10},{14,12},{16,14},{18,16},{20... | collective-permute-start | bytes 1179656 | tf_op jit(solution)/shard_map/ppermute | solution.py:27
  78.5 11.4 %collective-permute-start.2 = (bf16[256,768]{1,0:T(8,128)(2,1)S(1)}, bf16[256,768]{1,0:T(8,128)(2,1)S(1)}, u32[]{:S(2)}, u32[]{:S(2)}) collective-permute-start(bf16[256,768]{1,0:T(8,128)(2,1)S(1)} %collective-permute-done.1), channel_id=1, source_target_pairs={{0,2},{2,4},{4,6},{6,8},{8,10},{10,12},{12,14},{14,16},{16,18},{18... | collective-permute-start | bytes 1179656 | tf_op jit(solution)/shard_map/ppermute | solution.py:25
  89.9 14.8 %collective-permute-start.3 = (bf16[256,768]{1,0:T(8,128)(2,1)S(1)}, bf16[256,768]{1,0:T(8,128)(2,1)}, u32[]{:S(2)}, u32[]{:S(2)}) collective-permute-start(bf16[256,768]{1,0:T(8,128)(2,1)S(1)} %collective-permute-done.2), channel_id=1, source_target_pairs={{0,2},{2,4},{4,6},{6,8},{8,10},{10,12},{12,14},{14,16},{16,18},{18... | collective-permute-start | bytes 1179656 | tf_op jit(solution)/shard_map/ppermute | solution.py:25
  92.8 28.0 %collective-permute-start.10 = (bf16[256,768]{1,0:T(8,128)(2,1)S(1)}, bf16[256,768]{1,0:T(8,128)(2,1)S(1)}, u32[]{:S(2)}, u32[]{:S(2)}) collective-permute-start(bf16[256,768]{1,0:T(8,128)(2,1)S(1)} %collective-permute-done.9), channel_id=1, source_target_pairs={{2,0},{4,2},{6,4},{8,6},{10,8},{12,10},{14,12},{16,14},{18,16},{20... | collective-permute-start | bytes 1179656 | tf_op jit(solution)/shard_map/ppermute | solution.py:27
  104.7 18.1 %collective-permute-start.4 = (bf16[256,768]{1,0:T(8,128)(2,1)}, bf16[256,768]{1,0:T(8,128)(2,1)}, u32[]{:S(2)}, u32[]{:S(2)}) collective-permute-start(bf16[256,768]{1,0:T(8,128)(2,1)} %collective-permute-done.3), channel_id=1, source_target_pairs={{0,2},{2,4},{4,6},{6,8},{8,10},{10,12},{12,14},{14,16},{16,18},{18... | collective-permute-start | bytes 1179656 | tf_op jit(solution)/shard_map/ppermute | solution.py:25
  107.3 473.1 %reduce-scatter.14.cloned.1.call-start = ((), (), s32[]{:S(2)}) async-start(), calls=%async_computation.14 | async-start | bytes 13369344 | tf_op jit(solution)/shard_map/reduce_scatter | solution.py:215
  120.9 22.5 %collective-permute-start.11 = (bf16[256,768]{1,0:T(8,128)(2,1)S(1)}, bf16[256,768]{1,0:T(8,128)(2,1)}, u32[]{:S(2)}, u32[]{:S(2)}) collective-permute-start(bf16[256,768]{1,0:T(8,128)(2,1)S(1)} %collective-permute-done.10), channel_id=1, source_target_pairs={{2,0},{4,2},{6,4},{8,6},{10,8},{12,10},{14,12},{16,14},{18,16},{20... | collective-permute-start | bytes 1179656 | tf_op jit(solution)/shard_map/ppermute | solution.py:27
  122.8 20.6 %collective-permute-start.5 = (bf16[256,768]{1,0:T(8,128)(2,1)}, bf16[256,768]{1,0:T(8,128)(2,1)}, u32[]{:S(2)}, u32[]{:S(2)}) collective-permute-start(bf16[256,768]{1,0:T(8,128)(2,1)} %collective-permute-done.4), channel_id=1, source_target_pairs={{0,2},{2,4},{4,6},{6,8},{8,10},{10,12},{12,14},{14,16},{16,18},{18... | collective-permute-start | bytes 1179656 | tf_op jit(solution)/shard_map/ppermute | solution.py:25
  143.4 12.2 %collective-permute-start.12 = (bf16[256,768]{1,0:T(8,128)(2,1)}, bf16[256,768]{1,0:T(8,128)(2,1)}, u32[]{:S(2)}, u32[]{:S(2)}) collective-permute-start(bf16[256,768]{1,0:T(8,128)(2,1)} %collective-permute-done.11), channel_id=1, source_target_pairs={{2,0},{4,2},{6,4},{8,6},{10,8},{12,10},{14,12},{16,14},{18,16},{20... | collective-permute-start | bytes 1179656 | tf_op jit(solution)/shard_map/ppermute | solution.py:27
  143.4 12.2 %collective-permute-start.6 = (bf16[256,768]{1,0:T(8,128)(2,1)}, bf16[256,768]{1,0:T(8,128)(2,1)}, u32[]{:S(2)}, u32[]{:S(2)}) collective-permute-start(bf16[256,768]{1,0:T(8,128)(2,1)} %collective-permute-done.5), channel_id=1, source_target_pairs={{0,2},{2,4},{4,6},{6,8},{8,10},{10,12},{12,14},{14,16},{16,18},{18... | collective-permute-start | bytes 1179656 | tf_op jit(solution)/shard_map/ppermute | solution.py:25
  165.4 19.8 %collective-permute-start.14 = (bf16[256,768]{1,0:T(8,128)(2,1)}, bf16[256,768]{1,0:T(8,128)(2,1)S(1)}, u32[]{:S(2)}, u32[]{:S(2)}) collective-permute-start(bf16[256,768]{1,0:T(8,128)(2,1)} %collective-permute-done.13), channel_id=1, source_target_pairs={{2,0},{4,2},{6,4},{8,6},{10,8},{12,10},{14,12},{16,14},{18,16},{20... | collective-permute-start | bytes 1179656 | tf_op jit(solution)/shard_map/ppermute | solution.py:27
  446.4 158.5 %reduce-scatter.22.cloned.1.call-start = ((), (), s32[]{:S(2)}) async-start(), calls=%async_computation.18 | async-start | bytes 1769472
  474.0 154.9 %reduce-scatter.16.cloned.1.call-start = ((), (), s32[]{:S(2)}) async-start(), calls=%async_computation.15 | async-start | bytes 1769472 | tf_op jit(solution)/shard_map/reduce_scatter | solution.py:248
  475.5 216.2 %reduce-scatter.18.cloned.1.call-start = ((), (), s32[]{:S(2)}) async-start(), calls=%async_computation.16 | async-start | bytes 7077888 | tf_op jit(solution)/shard_map/reduce_scatter | solution.py:260
  480.8 273.8 %reduce-scatter.20.cloned.1.call-start = ((), (), s32[]{:S(2)}) async-start(), calls=%async_computation.17 | async-start | bytes 7077888 | tf_op jit(solution)/shard_map/reduce_scatter | solution.py:266
  486.5 292.7 %reduce-scatter.24.cloned.1.call-start = ((), (), s32[]{:S(2)}) async-start(), calls=%async_computation.19 | async-start | bytes 1769472
  583.4 220.4 %reduce-scatter.26.cloned.1.call-start = ((), (), s32[]{:S(2)}) async-start(), calls=%async_computation.20 | async-start | bytes 1769472
  (112 other events, 1775.5 us)
Sparse Core Ops, SparseCore 0:
  9.6 24.8 all-gather.20
  36.0 22.7 all-gather.18
  60.4 22.7 all-gather.16
  85.9 82.2 all-gather.22
  169.6 23.6 all-gather.24
  194.7 62.6 all-gather.26
  258.9 62.7 all-gather.28
  446.5 133.8 reduce-scatter.13
  583.2 21.6 reduce-scatter.21
  607.1 21.7 reduce-scatter.15
  631.8 59.9 reduce-scatter.17
  694.6 59.9 reduce-scatter.19
  757.5 21.7 reduce-scatter.23
  782.0 21.7 reduce-scatter.25
